TPU v7x, 32 devices: a whole 2x2x4 slice. The times are simulated.
32 devices in a mesh: wide: 8 (over z, y), narrow: 4 (over x, core).
Axes of the slice: x: 2, y: 2, z: 4, core: 2. Of those that a mesh axis runs over, the one named last changes fastest.
Arguments:
- passage_ids: int32 [64, 384], P(('wide', 'narrow')), may hold values from 0 to 17999
- query_ids: int32 [8, 32], P('wide'), may hold values from 0 to 17999
- passage_query: int32 [64], replicated, may hold values from -1 to 7, as said below
- kept_mask: int32 [64], replicated, may hold values 0 or 1
- neg_count: int32 [8], P('wide'), may hold values from 1 to 7, as said below
- step_count: int32 [1], replicated, may hold values from 2 to 20
- embed_table: float32 [18384, 768], P(None, ('wide', 'narrow')), may hold values from -6 to 6
- attend_in: float32 [2, 768, 2304], P(None, ('wide', 'narrow')), may hold values from -0.3125 to 0.3125
- attend_out: float32 [2, 768, 768], P(None, ('wide', 'narrow')), may hold values from -0.625 to 0.625
- expand_weight: float32 [2, 768, 3072], P(None, ('wide', 'narrow')), may hold values from -0.21875 to 0.21875
- shrink_weight: float32 [2, 3072, 768], P(None, ('wide', 'narrow')), may hold values from -0.109375 to 0.109375
- norm_gains: float32 [2, 3, 768], P(None, None, ('wide', 'narrow')), may hold values from 0.5 to 1.5
- bias_terms: float32 [2, 8448], P(None, ('wide', 'narrow')), may hold values from -0.6 to 0.6
- embed_first: float32 [18384, 768], P(None, ('wide', 'narrow')), may hold values from -3.7598107e-05 to 3.7598107e-05
- embed_second: float32 [18384, 768], P(None, ('wide', 'narrow')), may hold values from 1.59032e-12 to 2.544512e-11
- attend_in_first: float32 [2, 768, 2304], P(None, ('wide', 'narrow')), may hold values from -0.0001252017 to 0.0001252017
- attend_in_second: float32 [2, 768, 2304], P(None, ('wide', 'narrow')), may hold values from 1.7670223e-11 to 2.8272357e-10
- attend_out_first: float32 [2, 768, 768], P(None, ('wide', 'narrow')), may hold values from -0.0001252017 to 0.0001252017
- attend_out_second: float32 [2, 768, 768], P(None, ('wide', 'narrow')), may hold values from 1.7670223e-11 to 2.8272357e-10
- expand_first: float32 [2, 768, 3072], P(None, ('wide', 'narrow')), may hold values from -0.0001252017 to 0.0001252017
- expand_second: float32 [2, 768, 3072], P(None, ('wide', 'narrow')), may hold values from 1.7670223e-11 to 2.8272357e-10
- shrink_first: float32 [2, 3072, 768], P(None, ('wide', 'narrow')), may hold values from -0.0001252017 to 0.0001252017
- shrink_second: float32 [2, 3072, 768], P(None, ('wide', 'narrow')), may hold values from 1.7670223e-11 to 2.8272357e-10
- gains_first: float32 [2, 3, 768], P(None, None, ('wide', 'narrow')), may hold values from -0.0003759811 to 0.0003759811
- gains_second: float32 [2, 3, 768], P(None, None, ('wide', 'narrow')), may hold values from 1.59032e-10 to 2.544512e-09
- bias_first: float32 [2, 8448], P(None, ('wide', 'narrow')), may hold values from -0.0003759811 to 0.0003759811
- bias_second: float32 [2, 8448], P(None, ('wide', 'narrow')), may hold values from 1.59032e-10 to 2.544512e-09
Outputs:
- loss: float32 [], replicated
- grad_norm: float32 [], replicated
- embed_table_new: float32 [18384, 768], P(None, ('wide', 'narrow'))
- embed_first_new: float32 [18384, 768], P(None, ('wide', 'narrow'))
- embed_second_new: float32 [18384, 768], P(None, ('wide', 'narrow'))
- attend_in_new: float32 [2, 768, 2304], P(None, ('wide', 'narrow'))
- attend_in_first_new: float32 [2, 768, 2304], P(None, ('wide', 'narrow'))
- attend_in_second_new: float32 [2, 768, 2304], P(None, ('wide', 'narrow'))
- attend_out_new: float32 [2, 768, 768], P(None, ('wide', 'narrow'))
- attend_out_first_new: float32 [2, 768, 768], P(None, ('wide', 'narrow'))
- attend_out_second_new: float32 [2, 768, 768], P(None, ('wide', 'narrow'))
- expand_new: float32 [2, 768, 3072], P(None, ('wide', 'narrow'))
- expand_first_new: float32 [2, 768, 3072], P(None, ('wide', 'narrow'))
- expand_second_new: float32 [2, 768, 3072], P(None, ('wide', 'narrow'))
- shrink_new: float32 [2, 3072, 768], P(None, ('wide', 'narrow'))
- shrink_first_new: float32 [2, 3072, 768], P(None, ('wide', 'narrow'))
- shrink_second_new: float32 [2, 3072, 768], P(None, ('wide', 'narrow'))
- norm_gains_new: float32 [2, 3, 768], P(None, None, ('wide', 'narrow'))
- gains_first_new: float32 [2, 3, 768], P(None, None, ('wide', 'narrow'))
- gains_second_new: float32 [2, 3, 768], P(None, None, ('wide', 'narrow'))
- bias_terms_new: float32 [2, 8448], P(None, ('wide', 'narrow'))
- bias_first_new: float32 [2, 8448], P(None, ('wide', 'narrow'))
- bias_second_new: float32 [2, 8448], P(None, ('wide', 'narrow'))
Inputs may be any that keep to these rules, and one draw needn't show every extreme that they name: `passage_query`: slots from 0 hold the passages of query 0, then of query 1 and so on, each query 2 to 8 consecutive slots (the first is its positive), one query exactly 8, 40 slots in all; the remaining slots hold -1. `neg_count`: one less than the number of slots of that query in passage_query.
All inputs are finite; a program needn't handle non-finite values.
Results may differ from a plain program's by a relative error of at most 0.022.
The roundings to bfloat16 on the way count: a program that leaves them out, or rounds other values in their place, can miss the bound.
Values may be sent and summed in bfloat16 or wider, within the bound.
A program may use at most 448 MiB of HBM per device.

v0:
```python
from functools import partial

import jax
import jax.numpy as jnp
from jax import lax
from jax.sharding import PartitionSpec as P

D = 768
H = 12
HD = 64
FF = 3072
V = 18000
LP = 384


MARGIN = 1.0
CLIP = 1.0
BETA_ONE = 0.9
BETA_TWO = 0.999
LEARN_RATES = (1.0, 0.02, 0.08, 0.02, 0.02, 1.0, 0.1)
WEIGHT_DECAY = 0.01
ADAM_EPS = 1e-08
NORM_EPS = 1e-05


def merged(part, axis, combine):
    gathered = jax.tree.map(lambda a: lax.all_gather(a, axis), part)

    def take(source):
        return jax.tree.map(lambda a: lax.dynamic_index_in_dim(a, source, 0, False), gathered)

    return lax.fori_loop(
        1, lax.axis_size(axis), lambda source, state: combine(state, take(source)), take(0)
    )


def norm_layer(values, gain, shift):
    center = values - jnp.mean(values, axis=-1, keepdims=True)
    spread = jnp.mean(center * center, axis=-1, keepdims=True)
    return center * lax.rsqrt(spread + NORM_EPS) * gain + shift


def matmul(values, weight):
    return jnp.einsum("bli,ij->blj", values, weight, preferred_element_type=jnp.float32)


def matmul_back(values, weight):
    return jnp.einsum("blj,ij->bli", values, weight, preferred_element_type=jnp.float32)


def outer_sum(left, right):
    return jnp.einsum("bli,blj->ij", left, right, preferred_element_type=jnp.float32)


def encoder_forward(token_ids, weights, which):
    table, attend_in, attend_out, expand, shrink, gains, biases = weights
    batch, length = token_ids.shape
    gain = gains[which].astype(jnp.float32)
    bias = biases[which].astype(jnp.float32)
    embedded = (
        jnp.take(table, token_ids, axis=0).astype(jnp.float32)
        + table[V : V + length].astype(jnp.float32)[None]
    )
    normed = norm_layer(embedded, gain[0], bias[6 * D + FF :])
    normed_low = normed.astype(jnp.bfloat16)
    qkv_bias = jnp.concatenate([bias[0:D], jnp.zeros((D,), jnp.float32), bias[D : 2 * D]])
    packed = (matmul(normed_low, attend_in[which]) + qkv_bias).astype(jnp.bfloat16)
    heads = packed.reshape(batch, length, 3, H, HD)
    scores = (
        jnp.einsum(
            "bqhd,bkhd->bhqk", heads[:, :, 0], heads[:, :, 1], preferred_element_type=jnp.float32
        )
        * 0.125
    )
    peak = jnp.max(scores, axis=-1, keepdims=True)
    logsum = peak + jnp.log(jnp.sum(jnp.exp(scores - peak), axis=-1, keepdims=True))
    probs_low = jnp.exp(scores - logsum).astype(jnp.bfloat16)
    mixed = jnp.einsum(
        "bhqk,bkhd->bqhd", probs_low, heads[:, :, 2], preferred_element_type=jnp.float32
    )
    mixed_low = mixed.reshape(batch, length, D).astype(jnp.bfloat16)
    branch = matmul(mixed_low, attend_out[which]) + bias[2 * D : 3 * D]
    middle_in = normed + branch
    middle = norm_layer(middle_in, gain[1], bias[3 * D : 4 * D])
    middle_low = middle.astype(jnp.bfloat16)
    upper = matmul(middle_low, expand[which]) + bias[4 * D : 4 * D + FF]
    active_low = jax.nn.gelu(upper, approximate=False).astype(jnp.bfloat16)
    lower = matmul(active_low, shrink[which]) + bias[4 * D + FF : 5 * D + FF]
    top_in = middle + lower
    output = norm_layer(top_in, gain[2], bias[5 * D + FF : 6 * D + FF])
    cache = (
        embedded,
        normed_low,
        packed,
        logsum,
        mixed_low,
        middle_in,
        middle_low,
        upper,
        active_low,
        top_in,
    )
    return (output[:, 0].astype(jnp.bfloat16), cache)


def encoder_backward(token_ids, weights, which, cache, vec_grad):
    table, attend_in, attend_out, expand, shrink, gains, biases = weights
    (
        embedded,
        normed_low,
        packed,
        logsum,
        mixed_low,
        middle_in,
        middle_low,
        upper,
        active_low,
        top_in,
    ) = cache
    batch, length = token_ids.shape
    gain = gains[which].astype(jnp.float32)
    bias = biases[which].astype(jnp.float32)
    out_grad = jnp.concatenate(
        [vec_grad[:, None, :], jnp.zeros((batch, length - 1, D), jnp.float32)], axis=1
    )
    unused, pull_top = jax.vjp(norm_layer, top_in, gain[2], bias[5 * D + FF : 6 * D + FF])
    top_grad, gain_top, shift_top = pull_top(out_grad)
    lower_low = top_grad.astype(jnp.bfloat16)
    grad_shrink = outer_sum(active_low, lower_low)
    bias_lower = jnp.sum(lower_low.astype(jnp.float32), axis=(0, 1))
    active_grad = matmul_back(lower_low, shrink[which])
    unused, pull_gelu = jax.vjp(partial(jax.nn.gelu, approximate=False), upper)
    (upper_grad,) = pull_gelu(active_grad)
    upper_low = upper_grad.astype(jnp.bfloat16)
    grad_expand = outer_sum(middle_low, upper_low)
    bias_upper = jnp.sum(upper_low.astype(jnp.float32), axis=(0, 1))
    middle_grad = top_grad + matmul_back(upper_low, expand[which])
    unused, pull_mid = jax.vjp(norm_layer, middle_in, gain[1], bias[3 * D : 4 * D])
    inner_grad, gain_mid, shift_mid = pull_mid(middle_grad)
    branch_low = inner_grad.astype(jnp.bfloat16)
    grad_out = outer_sum(mixed_low, branch_low)
    bias_branch = jnp.sum(branch_low.astype(jnp.float32), axis=(0, 1))
    mixed_grad = (
        matmul_back(branch_low, attend_out[which])
        .astype(jnp.bfloat16)
        .reshape(batch, length, H, HD)
    )
    heads = packed.reshape(batch, length, 3, H, HD)
    queries = heads[:, :, 0]
    keyset = heads[:, :, 1]
    valueset = heads[:, :, 2]
    scores = (
        jnp.einsum("bqhd,bkhd->bhqk", queries, keyset, preferred_element_type=jnp.float32) * 0.125
    )
    probs = jnp.exp(scores - logsum)
    probs_low = probs.astype(jnp.bfloat16)
    value_grad = jnp.einsum(
        "bhqk,bqhd->bkhd", probs_low, mixed_grad, preferred_element_type=jnp.float32
    )
    prob_grad = jnp.einsum(
        "bqhd,bkhd->bhqk", mixed_grad, valueset, preferred_element_type=jnp.float32
    )
    score_low = (probs * (prob_grad - jnp.sum(prob_grad * probs, axis=-1, keepdims=True))).astype(
        jnp.bfloat16
    )
    query_grad = (
        jnp.einsum("bhqk,bkhd->bqhd", score_low, keyset, preferred_element_type=jnp.float32) * 0.125
    )
    key_grad = (
        jnp.einsum("bhqk,bqhd->bkhd", score_low, queries, preferred_element_type=jnp.float32)
        * 0.125
    )
    packed_low = (
        jnp.stack([query_grad, key_grad, value_grad], axis=2)
        .reshape(batch, length, 3 * D)
        .astype(jnp.bfloat16)
    )
    grad_in = outer_sum(normed_low, packed_low)
    packed_sum = jnp.sum(packed_low.astype(jnp.float32), axis=(0, 1))
    normed_grad = inner_grad + matmul_back(packed_low, attend_in[which])
    unused, pull_embed = jax.vjp(norm_layer, embedded, gain[0], bias[6 * D + FF :])
    embed_grad, gain_embed, shift_embed = pull_embed(normed_grad)
    gain_grad = jnp.stack([gain_embed, gain_mid, gain_top])
    bias_grad = jnp.concatenate(
        [
            packed_sum[0:D],
            packed_sum[2 * D : 3 * D],
            bias_branch,
            shift_mid,
            bias_upper,
            bias_lower,
            shift_top,
            shift_embed,
        ]
    )
    layer_grads = (grad_in, grad_out, grad_expand, grad_shrink, gain_grad, bias_grad)
    return (embed_grad, jnp.sum(embed_grad, axis=0), layer_grads)


def merge_stats(earlier, later):
    peak = jnp.maximum(earlier[0], later[0])
    total = earlier[1] * jnp.exp(earlier[0] - peak) + later[1] * jnp.exp(later[0] - peak)
    return (peak, total, earlier[2] + later[2])


def adam_update(weight, grad, first, second, step, rate):
    first_new = BETA_ONE * first + (1.0 - BETA_ONE) * grad
    second_new = BETA_TWO * second + (1.0 - BETA_TWO) * grad * grad
    first_hat = first_new / (1.0 - BETA_ONE**step)
    second_hat = second_new / (1.0 - BETA_TWO**step)
    weight_new = weight - rate * (
        first_hat / (jnp.sqrt(second_hat) + ADAM_EPS) + WEIGHT_DECAY * weight
    )
    return (weight_new, first_new, second_new)


def on_device(
    passage_ids,
    query_ids,
    passage_query,
    kept_mask,
    neg_count,
    step_count,
    embed_table,
    attend_in,
    attend_out,
    expand_weight,
    shrink_weight,
    norm_gains,
    bias_terms,
    embed_first,
    embed_second,
    attend_in_first,
    attend_in_second,
    attend_out_first,
    attend_out_second,
    expand_first,
    expand_second,
    shrink_first,
    shrink_second,
    gains_first,
    gains_second,
    bias_first,
    bias_second,
):
    masters = (
        embed_table,
        attend_in,
        attend_out,
        expand_weight,
        shrink_weight,
        norm_gains,
        bias_terms,
    )
    full = (
        lax.all_gather(embed_table.astype(jnp.bfloat16), ("wide", "narrow"), axis=1, tiled=True),
        lax.all_gather(attend_in.astype(jnp.bfloat16), ("wide", "narrow"), axis=1, tiled=True),
        lax.all_gather(attend_out.astype(jnp.bfloat16), ("wide", "narrow"), axis=1, tiled=True),
        lax.all_gather(expand_weight.astype(jnp.bfloat16), ("wide", "narrow"), axis=1, tiled=True),
        lax.all_gather(shrink_weight.astype(jnp.bfloat16), ("wide", "narrow"), axis=1, tiled=True),
        lax.all_gather(norm_gains.astype(jnp.bfloat16), ("wide", "narrow"), axis=2, tiled=True),
        lax.all_gather(bias_terms.astype(jnp.bfloat16), ("wide", "narrow"), axis=1, tiled=True),
    )
    query_vecs, query_cache = encoder_forward(query_ids, full, 0)
    passage_vecs, passage_cache = encoder_forward(passage_ids, full, 1)
    passage_block = lax.all_gather(passage_vecs, "wide", axis=0, tiled=True)
    wide_count = lax.axis_size("wide")
    narrow_count = lax.axis_size("narrow")
    wide_at = lax.axis_index("wide")
    narrow_at = lax.axis_index("narrow")
    per_device = passage_ids.shape[0]
    per_wide = query_ids.shape[0]
    slots = (
        (jnp.arange(wide_count, dtype=jnp.int32)[:, None] * narrow_count + narrow_at) * per_device
        + jnp.arange(per_device, dtype=jnp.int32)[None, :]
    ).reshape(-1)
    earlier = jnp.concatenate([jnp.full((1,), -1, jnp.int32), passage_query[:-1]])
    first_slot = (passage_query >= 0) & (passage_query != earlier)
    tile_owner = jnp.take(passage_query, slots)
    tile_first = jnp.take(first_slot, slots)
    tile_kept = jnp.take(kept_mask, slots) == 1
    query_index = wide_at * per_wide + jnp.arange(per_wide, dtype=jnp.int32)
    member = tile_owner[None, :] == query_index[:, None]
    positive = member & tile_first[None, :]
    negative = member & jnp.logical_not(tile_first)[None, :] & tile_kept[None, :]
    valid = (tile_owner >= 0)[None, :]
    score_scale = 2.0 * D ** (-0.5)
    scores = (
        jnp.einsum("qd,pd->qp", query_vecs, passage_block, preferred_element_type=jnp.float32)
        * score_scale
    )
    masked = jnp.where(valid, scores, -1e30)
    peak = jnp.max(masked, axis=1)
    summed = jnp.sum(jnp.where(valid, jnp.exp(masked - peak[:, None]), 0.0), axis=1)
    pos_part = jnp.sum(jnp.where(positive, scores, 0.0), axis=1)
    peak, summed, pos_score = merged((peak, summed, pos_part), "narrow", merge_stats)
    logsum = peak + jnp.log(summed)
    margins = MARGIN - pos_score[:, None] + scores
    active = negative & (margins > 0)
    counts = neg_count.astype(jnp.float32)
    hinge = jnp.sum(jnp.where(active, margins, 0.0), axis=1) / counts
    active_total = lax.psum(jnp.sum(active.astype(jnp.float32), axis=1), "narrow")
    query_keep = (narrow_at == 0).astype(jnp.float32)
    loss_part = jnp.sum(query_keep * (logsum - pos_score) + hinge)
    loss = lax.psum(loss_part, ("wide", "narrow"))
    score_grad = (
        jnp.where(valid, jnp.exp(scores - logsum[:, None]), 0.0)
        - positive.astype(jnp.float32) * (1.0 + active_total / counts)[:, None]
        + active.astype(jnp.float32) / counts[:, None]
    )
    score_low = score_grad.astype(jnp.bfloat16)
    query_part = (
        jnp.einsum("qp,pd->qd", score_low, passage_block, preferred_element_type=jnp.float32)
        * score_scale
    )
    passage_part = (
        jnp.einsum("qp,qd->pd", score_low, query_vecs, preferred_element_type=jnp.float32)
        * score_scale
    )
    query_grad = lax.psum(query_part, "narrow").astype(jnp.bfloat16).astype(jnp.float32)
    passage_grad = (
        lax.psum_scatter(passage_part, "wide", scatter_dimension=0, tiled=True)
        .astype(jnp.bfloat16)
        .astype(jnp.float32)
    )
    query_embed, query_pos, query_layer = encoder_backward(
        query_ids, full, 0, query_cache, query_grad
    )
    passage_embed, passage_pos, passage_layer = encoder_backward(
        passage_ids, full, 1, passage_cache, passage_grad
    )
    rows = jnp.concatenate([query_ids.reshape(-1), passage_ids.reshape(-1)])
    row_values = jnp.concatenate(
        [(query_embed * query_keep).reshape(-1, D), passage_embed.reshape(-1, D)]
    )
    table_grad = jax.ops.segment_sum(row_values, rows, num_segments=V + LP)
    table_grad = table_grad.at[V : V + query_ids.shape[1]].add(query_pos * query_keep)
    table_grad = table_grad.at[V : V + passage_ids.shape[1]].add(passage_pos)
    stacked = [
        jnp.stack([query_layer[index] * query_keep, passage_layer[index]]) for index in range(6)
    ]
    reduced = (
        lax.psum_scatter(table_grad, ("wide", "narrow"), scatter_dimension=1, tiled=True),
        lax.psum_scatter(stacked[0], ("wide", "narrow"), scatter_dimension=1, tiled=True),
        lax.psum_scatter(stacked[1], ("wide", "narrow"), scatter_dimension=1, tiled=True),
        lax.psum_scatter(stacked[2], ("wide", "narrow"), scatter_dimension=1, tiled=True),
        lax.psum_scatter(stacked[3], ("wide", "narrow"), scatter_dimension=1, tiled=True),
        lax.psum_scatter(stacked[4], ("wide", "narrow"), scatter_dimension=2, tiled=True),
        lax.psum_scatter(stacked[5], ("wide", "narrow"), scatter_dimension=1, tiled=True),
    )
    local_squares = jnp.zeros((), jnp.float32)
    for grad_piece in reduced:
        local_squares = local_squares + jnp.sum(grad_piece * grad_piece)
    squares = lax.psum(local_squares, ("wide", "narrow"))
    grad_norm = jnp.sqrt(squares)
    factor = CLIP / jnp.maximum(grad_norm, CLIP)
    step = step_count[0].astype(jnp.float32)
    firsts = (
        embed_first,
        attend_in_first,
        attend_out_first,
        expand_first,
        shrink_first,
        gains_first,
        bias_first,
    )
    seconds = (
        embed_second,
        attend_in_second,
        attend_out_second,
        expand_second,
        shrink_second,
        gains_second,
        bias_second,
    )
    results = [loss, grad_norm]
    for index in range(7):
        weight_new, first_new, second_new = adam_update(
            masters[index],
            reduced[index] * factor,
            firsts[index],
            seconds[index],
            step,
            LEARN_RATES[index],
        )
        results.extend([weight_new, first_new, second_new])
    return tuple(results)


def solution(mesh):
    in_specs = (
        P(("wide", "narrow"), None),
        P("wide", None),
        P(),
        P(),
        P("wide"),
        P(),
        P(None, ("wide", "narrow")),
        P(None, ("wide", "narrow"), None),
        P(None, ("wide", "narrow"), None),
        P(None, ("wide", "narrow"), None),
        P(None, ("wide", "narrow"), None),
        P(None, None, ("wide", "narrow")),
        P(None, ("wide", "narrow")),
        P(None, ("wide", "narrow")),
        P(None, ("wide", "narrow")),
        P(None, ("wide", "narrow"), None),
        P(None, ("wide", "narrow"), None),
        P(None, ("wide", "narrow"), None),
        P(None, ("wide", "narrow"), None),
        P(None, ("wide", "narrow"), None),
        P(None, ("wide", "narrow"), None),
        P(None, ("wide", "narrow"), None),
        P(None, ("wide", "narrow"), None),
        P(None, None, ("wide", "narrow")),
        P(None, None, ("wide", "narrow")),
        P(None, ("wide", "narrow")),
        P(None, ("wide", "narrow")),
    )
    out_specs = (
        P(),
        P(),
        P(None, ("wide", "narrow")),
        P(None, ("wide", "narrow")),
        P(None, ("wide", "narrow")),
        P(None, ("wide", "narrow"), None),
        P(None, ("wide", "narrow"), None),
        P(None, ("wide", "narrow"), None),
        P(None, ("wide", "narrow"), None),
        P(None, ("wide", "narrow"), None),
        P(None, ("wide", "narrow"), None),
        P(None, ("wide", "narrow"), None),
        P(None, ("wide", "narrow"), None),
        P(None, ("wide", "narrow"), None),
        P(None, ("wide", "narrow"), None),
        P(None, ("wide", "narrow"), None),
        P(None, ("wide", "narrow"), None),
        P(None, None, ("wide", "narrow")),
        P(None, None, ("wide", "narrow")),
        P(None, None, ("wide", "narrow")),
        P(None, ("wide", "narrow")),
        P(None, ("wide", "narrow")),
        P(None, ("wide", "narrow")),
    )
    return jax.shard_map(
        on_device, mesh=mesh, in_specs=in_specs, out_specs=out_specs, check_vma=False
    )
```

profile of v0, /device:TPU:0, one launch (start us, length us, event | category | flops | bytes accessed | tf_op | source)
XLA Modules:
  0.0 2339.9 jit_solution(517223260094500574)
XLA Ops:
  16.7 44.6 %all-gather.1 = bf16[32,264,2]{1,2,0:T(2,128)(2,1)S(1)} all-gather(bf16[1,264,2]{1,2,0:T(2,128)(2,1)S(1)} %convert_bitcast_fusion.1), channel_id=1, replica_groups=mesh['wide'=8,'narrow'=4] {'wide','narrow'}, dimensions={0}, use_global_device_ids=true | all-gather | bytes 34848 | tf_op jit(solution)/shard_map/all_gather | solution.py:262
  65.5 39.6 %all_gather.43 = bf16[2,3,768]{1,0,2:T(2,128)(2,1)S(1)} all-gather(bf16[2,3,24]{1,0,2:T(2,128)(2,1)S(1)} %copy.214), channel_id=1, replica_groups=mesh['wide'=8,'narrow'=4] {'wide','narrow'}, dimensions={2}, use_global_device_ids=true | all-gather | bytes 9504 | tf_op jit(solution)/shard_map/all_gather | solution.py:261
  106.4 12.5 slice_reduce_fusion
  119.0 68.1 %all-gather.8.cloned.1.call-done = bf16[18384,768]{0,1:T(8,128)(2,1)} async-done(((bf16[18384,24]{0,1:T(8,128)(2,1)}), bf16[18384,768]{0,1:T(8,128)(2,1)}) %all-gather.8.cloned.1.call-update) | async-done | bytes 28237840 | tf_op jit(solution)/shard_map/all_gather | solution.py:256
  188.9 37.5 %copy.212 = bf16[18384,768]{1,0:T(8,128)(2,1)} copy(bf16[18384,768]{0,1:T(8,128)(2,1)} %all-gather.8.cloned.1.call-done) | data formatting | bytes 56475648 | tf_op jit(solution)/shard_map/all_gather | solution.py:256
  226.4 13.8 gather_fusion
  242.3 18.5 all-gather.10.cloned.1.call-done
  265.2 54.6 %all-gather.12.cloned.1.call-done = bf16[2,768,768]{2,1,0:T(8,128)(2,1)} async-done(((bf16[2,24,768]{2,1,0:T(8,128)(2,1)}), bf16[2,768,768]{2,1,0:T(8,128)(2,1)}) %all-gather.12.cloned.1.call-update) | async-done | bytes 2359312 | tf_op jit(solution)/shard_map/all_gather | solution.py:258
  321.8 81.8 %all-gather.14.cloned.1.call-done = bf16[2,768,3072]{2,1,0:T(8,128)(2,1)} async-done(((bf16[2,24,3072]{2,1,0:T(8,128)(2,1)}), bf16[2,768,3072]{2,1,0:T(8,128)(2,1)}) %all-gather.14.cloned.1.call-update) | async-done | bytes 9437200 | tf_op jit(solution)/shard_map/all_gather | solution.py:259
  407.0 80.1 %all-gather.16.cloned.1.call-done = bf16[2,3072,768]{2,1,0:T(8,128)(2,1)} async-done(((bf16[2,96,768]{2,1,0:T(8,128)(2,1)}), bf16[2,3072,768]{2,1,0:T(8,128)(2,1)}) %all-gather.16.cloned.1.call-update) | async-done | bytes 9437200 | tf_op jit(solution)/shard_map/all_gather | solution.py:260
  492.2 16.0 gather_fusion.1
  510.1 6.8 add_convert_fusion.1
  517.0 4.6 copy.223
  521.6 6.4 multiply_reduce_fusion.1
  528.0 7.5 exponential_reduce_fusion
  535.6 7.8 convolution_convert_fusion
  546.2 9.3 fusion.28
  555.5 23.1 multiply_convert_fusion.1
  578.6 8.1 fusion.142
  587.9 30.8 %all-gather = bf16[16,1,768]{2,1,0:T(2,128)(2,1)S(1)} all-gather(bf16[2,1,768]{2,1,0:T(2,128)(2,1)S(1)} %fusion.92), channel_id=2, replica_groups=mesh['wide'=8,'narrow'=4] {'wide'}, dimensions={0}, use_global_device_ids=true | all-gather | bytes 27648 | tf_op jit(solution)/shard_map/all_gather | solution.py:266
  625.0 5.7 all-reduce.11
  630.8 11.7 while.21
  643.1 7.2 psum.29
  651.1 10.8 psum.30
  663.5 4.7 convert_reduce_fusion.6
  676.1 35.5 %all-reduce.5 = bf16[16,768]{1,0:T(8,128)(2,1)S(1)} all-reduce(f32[16,768]{1,0:T(8,128)S(1)} %multiply_multiply_fusion.15), channel_id=3, replica_groups=mesh['wide'=8,'narrow'=4] {'wide'}, use_global_device_ids=true, to_apply=%region_33.35.clone | all-reduce | flops 12288 | bytes 73728
  716.9 12.9 convert_reduce_fusion
  729.8 9.4 multiply_reduce_fusion.3
  752.3 14.5 multiply_reduce_fusion
  766.8 7.3 multiply_convert_fusion
  782.8 5.3 multiply_bitcast_fusion.2
  788.2 6.5 convolution_bitcast_fusion
  794.8 11.7 pad_maximum_fusion.2
  809.6 5.9 convolution_bitcast_fusion.1
  815.5 6.9 pad_maximum_fusion.1
  825.0 6.7 convolution_bitcast_fusion.2
  831.7 6.7 pad_maximum_fusion
  841.4 7.8 fusion.122
  861.4 34.7 %scatter_custom_fusion = f32[18384,768]{1,0:T(8,128)} fusion(s32[800]{0:T(1024)} %pad_add_fusion, f32[800,768]{1,0:T(8,128)} %pad_maximum_fusion.4, f32[]{:T(128)} %constant.171.clone.1), kind=kCustom, calls=%fused_computation.9 | custom fusion | flops 614400 | bytes 56476160 | tf_op jit(solution)/shard_map/scatter-add | solution.py:336
  902.9 41.2 %all-reduce.7 = f32[2,3,768]{2,1,0:T(4,128)S(1)} all-reduce(f32[2,3,768]{2,1,0:T(4,128)S(1)} %pad_maximum_fusion.6), channel_id=9, replica_groups=mesh['wide'=8,'narrow'=4] {'wide','narrow'}, use_global_device_ids=true, to_apply=%region_59.61.clone | all-reduce | flops 4608 | bytes 36864
  946.3 78.6 %reduce-scatter.8.cloned.1.call-done = f32[2,24,2304]{2,1,0:T(8,128)} async-done(((f32[2,768,2304]{2,1,0:T(8,128)}), f32[2,24,2304]{2,1,0:T(8,128)}) %reduce-scatter.8.cloned.1.call-update) | async-done | bytes 442384 | tf_op jit(solution)/shard_map/reduce_scatter | solution.py:344
  1026.7 209.3 %reduce-scatter.14.cloned.1.call-done = f32[2,96,768]{2,1,0:T(8,128)} async-done(((f32[2,3072,768]{2,1,0:T(8,128)}), f32[2,96,768]{2,1,0:T(8,128)}) %reduce-scatter.14.cloned.1.call-update) | async-done | bytes 589840 | tf_op jit(solution)/shard_map/reduce_scatter | solution.py:347
  1237.7 208.8 %reduce-scatter.12.cloned.1.call-done = f32[2,24,3072]{2,1,0:T(8,128)} async-done(((f32[2,768,3072]{2,1,0:T(8,128)}), f32[2,24,3072]{2,1,0:T(8,128)}) %reduce-scatter.12.cloned.1.call-update) | async-done | bytes 589840 | tf_op jit(solution)/shard_map/reduce_scatter | solution.py:346
  1448.3 802.8 %all-reduce.14.cloned.1.call-done = (f32[18384,768]{1,0:T(8,128)}, f32[2,8448]{1,0:T(2,128)}) async-done(((f32[18384,768]{1,0:T(8,128)}, f32[2,8448]{1,0:T(2,128)}), (f32[18384,768]{1,0:T(8,128)}, f32[2,8448]{1,0:T(2,128)})) %all-reduce.14.cloned.1.call-update) | async-done | bytes 56543248
  2251.1 12.1 multiply_reduce_fusion.2
  2263.2 5.6 copy.244
  2274.8 40.8 %all-reduce.9 = (f32[]{:T(128)}, f32[]{:T(128)}) all-reduce(f32[]{:T(128)} %bitcast.47, f32[]{:T(128)S(6)} %add.643), channel_id=1, replica_groups=mesh['wide'=8,'narrow'=4] {'wide','narrow'}, use_global_device_ids=true, to_apply=%region_22.24 | all-reduce | flops 2 | bytes 16 | tf_op jit(solution)/shard_map/psum | solution.py:305
  2320.3 5.5 add_subtract_fusion
  (598 shorter events, 128.6 us)
Async XLA Ops:
  7.3 179.8 %all-gather.8.cloned.1.call-start = ((), (), s32[]{:S(2)}) async-start(), calls=%async_computation.4 | async-start | bytes 29196288 | tf_op jit(solution)/shard_map/all_gather | solution.py:256
  9.9 250.9 %all-gather.10.cloned.1.call-start = ((), (), s32[]{:S(2)}) async-start(), calls=%async_computation.5 | async-start | bytes 7299072 | tf_op jit(solution)/shard_map/all_gather | solution.py:257
  10.7 51.5 %copy-start.180 = (u32[32]{0:T(128)S(1)}, u32[32]{0:T(128)}, u32[]{:S(2)}) copy-start(u32[32]{0:T(128)} %constant.436) | copy-start | bytes 388
  10.7 52.8 %copy-start.179 = (u32[32]{0:T(128)S(1)}, u32[32]{0:T(128)}, u32[]{:S(2)}) copy-start(u32[32]{0:T(128)} %constant.418) | copy-start | bytes 388
  10.7 309.1 %all-gather.12.cloned.1.call-start = ((), (), s32[]{:S(2)}) async-start(), calls=%async_computation.6 | async-start | bytes 2433024 | tf_op jit(solution)/shard_map/all_gather | solution.py:258
  11.5 93.6 %copy-start.174 = (s32[1,32]{1,0:T(1,128)S(1)}, s32[1,32]{1,0:T(1,128)}, u32[]{:S(2)}) copy-start(s32[1,32]{1,0:T(1,128)} %param.36) | copy-start | bytes 388
  11.5 392.2 %all-gather.14.cloned.1.call-start = ((), (), s32[]{:S(2)}) async-start(), calls=%async_computation.7 | async-start | bytes 9732096 | tf_op jit(solution)/shard_map/all_gather | solution.py:259
  12.3 474.8 %all-gather.16.cloned.1.call-start = ((), (), s32[]{:S(2)}) async-start(), calls=%async_computation.8 | async-start | bytes 9732096 | tf_op jit(solution)/shard_map/all_gather | solution.py:260
  13.1 931.6 %reduce-scatter.10.cloned.1.call-start = ((), (), s32[]{:S(2)}) async-start(), calls=%async_computation.10 | async-start | bytes 4866048 | tf_op jit(solution)/shard_map/reduce_scatter | solution.py:345
  13.4 105.6 %copy-start.149 = (s32[16]{0:T(128)}, s32[16]{0:T(128)S(1)}, u32[]{:S(2)}) copy-start(s32[16]{0:T(128)S(1)} %add.573) | copy-start | bytes 196
  105.8 214.0 %copy-start.87 = (f32[768]{0:T(1024)}, f32[768]{0:T(1024)S(1)}, u32[]{:S(2)}) copy-start(f32[768]{0:T(1024)S(1)} %get-tuple-element.501) | copy-start | bytes 9220
  105.8 381.3 %copy-start.82 = (f32[768]{0:T(1024)}, f32[768]{0:T(1024)S(1)}, u32[]{:S(2)}) copy-start(f32[768]{0:T(1024)S(1)} %get-tuple-element.505) | copy-start | bytes 9220
  105.8 403.8 %copy-start.154 = (f32[768]{0:T(1024)}, f32[768]{0:T(1024)S(1)}, u32[]{:S(2)}) copy-start(f32[768]{0:T(1024)S(1)} %get-tuple-element.381) | copy-start | bytes 9220
  105.8 214.0 %copy-start.113 = (pred[32]{0:T(512)(128)(4,1)}, pred[32]{0:T(512)(128)(4,1)S(1)}, u32[]{:S(2)}) copy-start(pred[32]{0:T(512)(128)(4,1)S(1)} %and_bitcast_fusion) | copy-start | bytes 100
  105.9 403.7 %copy-start.98 = (pred[2,384]{1,0:T(4,128)(4,1)}, pred[2,384]{1,0:T(4,128)(4,1)S(1)}, u32[]{:S(2)}) copy-start(pred[2,384]{1,0:T(4,128)(4,1)S(1)} %compare_and_fusion) | copy-start | bytes 2308
  119.0 200.9 %copy-start.72 = (f32[768]{0:T(1024)}, f32[768]{0:T(1024)S(1)}, u32[]{:S(2)}) copy-start(f32[768]{0:T(1024)S(1)} %get-tuple-element.508) | copy-start | bytes 9220
  119.0 368.1 %copy-start.69 = (f32[768]{0:T(1024)}, f32[768]{0:T(1024)S(1)}, u32[]{:S(2)}) copy-start(f32[768]{0:T(1024)S(1)} %get-tuple-element.509) | copy-start | bytes 9220
  119.0 390.6 %copy-start.101 = (f32[768]{0:T(1024)}, f32[768]{0:T(1024)S(1)}, u32[]{:S(2)}) copy-start(f32[768]{0:T(1024)S(1)} %get-tuple-element.360) | copy-start | bytes 9220
  188.9 320.7 %copy-start.8 = (f32[384,768]{1,0:T(8,128)}, f32[384,768]{1,0:T(8,128)S(1)}, u32[]{:S(2)}) copy-start(f32[384,768]{1,0:T(8,128)S(1)} %copy.222) | copy-start | bytes 3538948
  240.2 79.6 %copy-start.29 = (bf16[32,768]{1,0:T(8,128)(2,1)}, bf16[32,768]{1,0:T(8,128)(2,1)S(1)}, u32[]{:S(2)}) copy-start(bf16[32,768]{1,0:T(8,128)(2,1)S(1)} %gather_fusion) | copy-start | bytes 147460
  241.3 78.6 %copy-start.127 = (f32[32]{0:T(128)}, f32[32]{0:T(128)S(1)}, u32[]{:S(2)}) copy-start(f32[32]{0:T(128)S(1)} %broadcast_multiply_fusion.7) | copy-start | bytes 388
  242.3 77.6 %copy-start.129 = (f32[32]{0:T(128)}, f32[32]{0:T(128)S(1)}, u32[]{:S(2)}) copy-start(f32[32]{0:T(128)S(1)} %fusion.107) | copy-start | bytes 388
  263.9 143.1 %copy-start.48 = (bf16[1,32,1,12,64]{4,3,2,1,0:T(8,128)(2,1)}, bf16[1,32,1,12,64]{4,3,2,1,0:T(8,128)(2,1)S(1)}, u32[]{:S(2)}) copy-start(bf16[1,32,1,12,64]{4,3,2,1,0:T(8,128)(2,1)S(1)} %get-tuple-element.463) | copy-start | bytes 147460
  263.9 143.1 %copy-start.50 = (bf16[1,32,1,12,64]{4,3,2,1,0:T(8,128)(2,1)}, bf16[1,32,1,12,64]{4,3,2,1,0:T(8,128)(2,1)S(1)}, u32[]{:S(2)}) copy-start(bf16[1,32,1,12,64]{4,3,2,1,0:T(8,128)(2,1)S(1)} %get-tuple-element.461) | copy-start | bytes 147460
  263.9 143.0 %copy-start.52 = (bf16[1,32,1,12,64]{4,3,2,1,0:T(8,128)(2,1)}, bf16[1,32,1,12,64]{4,3,2,1,0:T(8,128)(2,1)S(1)}, u32[]{:S(2)}) copy-start(bf16[1,32,1,12,64]{4,3,2,1,0:T(8,128)(2,1)S(1)} %get-tuple-element.462) | copy-start | bytes 147460
  265.2 141.8 %copy-start.78 = (bf16[32,768]{1,0:T(8,128)(2,1)}, bf16[32,768]{1,0:T(8,128)(2,1)S(1)}, u32[]{:S(2)}) copy-start(bf16[32,768]{1,0:T(8,128)(2,1)S(1)} %convert_element_type.286) | copy-start | bytes 147460
  321.6 165.5 %copy-start.31 = (f32[32,768]{1,0:T(8,128)}, f32[32,768]{1,0:T(8,128)S(1)}, u32[]{:S(2)}) copy-start(f32[32,768]{1,0:T(8,128)S(1)} %get-tuple-element.484) | copy-start | bytes 294916
  321.6 165.5 %copy-start.131 = (f32[32]{0:T(128)}, f32[32]{0:T(128)S(1)}, u32[]{:S(2)}) copy-start(f32[32]{0:T(128)S(1)} %broadcast_multiply_fusion.6) | copy-start | bytes 388
  321.8 85.2 %copy-start.168 = (f32[32]{0:T(128)}, f32[32]{0:T(128)S(1)}, u32[]{:S(2)}) copy-start(f32[32]{0:T(128)S(1)} %multiply_reduce_fusion.16) | copy-start | bytes 388
  321.8 165.3 %copy-start.144 = (f32[32]{0:T(128)}, f32[32]{0:T(128)S(1)}, u32[]{:S(2)}) copy-start(f32[32]{0:T(128)S(1)} %fusion.108) | copy-start | bytes 388
  407.0 84.0 %copy-start.64 = (f32[32,3072]{1,0:T(8,128)}, f32[32,3072]{1,0:T(8,128)S(1)}, u32[]{:S(2)}) copy-start(f32[32,3072]{1,0:T(8,128)S(1)} %fusion.16) | copy-start | bytes 1179652
  545.9 193.3 %copy-start.76 = (f32[2,384]{1,0:T(2,128)}, f32[2,384]{1,0:T(2,128)S(1)}, u32[]{:S(2)}) copy-start(f32[2,384]{1,0:T(2,128)S(1)} %fusion.100) | copy-start | bytes 9220
  587.3 55.2 %copy-start.165 = (s32[16]{0:T(128)S(1)}, s32[16]{0:T(128)}, u32[]{:S(2)}) copy-start(s32[16]{0:T(128)} %gather_fusion.4) | copy-start | bytes 196
  587.3 75.3 %copy-start.173 = (f32[32]{0:T(128)S(1)}, f32[32]{0:T(128)}, u32[]{:S(2)}) copy-start(f32[32]{0:T(128)} %copy-done.172) | copy-start | bytes 388
  587.3 76.2 %copy-start.65 = (f32[32,3072]{1,0:T(8,128)S(1)}, f32[32,3072]{1,0:T(8,128)}, u32[]{:S(2)}) copy-start(f32[32,3072]{1,0:T(8,128)} %copy-done.64) | copy-start | bytes 1179652
  673.8 39.1 %copy-start.170 = (f32[32]{0:T(128)}, f32[32]{0:T(128)S(1)}, u32[]{:S(2)}) copy-start(f32[32]{0:T(128)S(1)} %negate_multiply_fusion.6) | copy-start | bytes 388
  674.5 38.4 %copy-start.79 = (bf16[1,32,768]{2,1,0:T(8,128)(2,1)}, bf16[1,32,768]{2,1,0:T(8,128)(2,1)S(1)}, u32[]{:S(2)}) copy-start(bf16[1,32,768]{2,1,0:T(8,128)(2,1)S(1)} %get-tuple-element.437) | copy-start | bytes 147460
  750.3 274.6 %reduce-scatter.8.cloned.1.call-start = ((), (), s32[]{:S(2)}) async-start(), calls=%async_computation.9 | async-start | bytes 14598144 | tf_op jit(solution)/shard_map/reduce_scatter | solution.py:344
  806.5 429.4 %reduce-scatter.14.cloned.1.call-start = ((), (), s32[]{:S(2)}) async-start(), calls=%async_computation.12 | async-start | bytes 19464192 | tf_op jit(solution)/shard_map/reduce_scatter | solution.py:347
  822.4 624.1 %reduce-scatter.12.cloned.1.call-start = ((), (), s32[]{:S(2)}) async-start(), calls=%async_computation.11 | async-start | bytes 19464192 | tf_op jit(solution)/shard_map/reduce_scatter | solution.py:346
  838.5 1412.6 %all-reduce.14.cloned.1.call-start = ((), (), s32[]{:S(2)}) async-start(), calls=%async_computation.13 | async-start | bytes 113086464
  861.4 34.9 %copy-start.162 = (f32[768]{0:T(1024)S(1)}, f32[768]{0:T(1024)}, u32[]{:S(2)}) copy-start(f32[768]{0:T(1024)} %get-tuple-element.365) | copy-start | bytes 9220
  861.4 34.9 %copy-start.47 = (f32[32,768]{1,0:T(8,128)S(1)}, f32[32,768]{1,0:T(8,128)}, u32[]{:S(2)}) copy-start(f32[32,768]{1,0:T(8,128)} %copy-done.46) | copy-start | bytes 294916
  944.1 1319.1 %copy-start.97 = (f32[2,3,768]{2,1,0:T(4,128)}, f32[2,3,768]{2,1,0:T(4,128)S(1)}, u32[]{:S(2)}) copy-start(f32[2,3,768]{2,1,0:T(4,128)S(1)} %all-reduce.7) | copy-start | bytes 55300
  2263.2 53.1 %copy-start.137 = (f32[2,3,24]{2,0,1:T(2,128)S(1)}, f32[2,3,24]{2,0,1:T(2,128)}, u32[]{:S(2)}) copy-start(f32[2,3,24]{2,0,1:T(2,128)} %param.46) | copy-start | bytes 1732
  2263.2 53.1 %copy-start.164 = (f32[2,3,24]{2,0,1:T(2,128)S(1)}, f32[2,3,24]{2,0,1:T(2,128)}, u32[]{:S(2)}) copy-start(f32[2,3,24]{2,0,1:T(2,128)} %param.59) | copy-start | bytes 1732
  2263.2 55.6 %copy-start.143 = (f32[2,264]{1,0:T(2,128)S(1)}, f32[2,264]{1,0:T(2,128)}, u32[]{:S(2)}) copy-start(f32[2,264]{1,0:T(2,128)} %param.47) | copy-start | bytes 6340
  2263.2 57.0 %copy-start.17 = (f32[18384,24]{0,1:T(8,128)S(1)}, f32[18384,24]{0,1:T(8,128)}, u32[]{:S(2)}) copy-start(f32[18384,24]{0,1:T(8,128)} %param.41) | copy-start | bytes 5294596
  (147 other events, 1191.9 us)
Sparse Core Ops, SparseCore 0:
  11.5 175.5 all-gather.7
  190.6 70.1 all-gather.9
  264.3 55.4 all-gather.11
  323.2 80.3 all-gather.13
  407.0 80.0 all-gather.15
  750.4 104.9 reduce-scatter.9
  861.4 163.4 reduce-scatter.7
  1031.3 204.5 reduce-scatter.13
  1242.3 204.1 reduce-scatter.11
  1453.3 797.7 all-reduce.13
where the time goes:
time: 2350 us; the launch traced here: 2340 us
  waiting for transfers between devices  1600 us (68%)
  blocking collectives  256 us (11%)
  other arithmetic  172 us (7%)
  matrix products  150 us (6%)
  local copies, waits for them, and re-layouts  123 us (5%)
  between operations  27 us (1%)
    unnamed x11, waiting for transfers between devices  803 us
    reduce_scatter x1, waiting for transfers between devices, on_device(): lax.psum_scatter(stacked[3], ('wide', 'narrow'), scatter_dimension=1, til...  209 us
    reduce_scatter x1, waiting for transfers between devices, on_device(): lax.psum_scatter(stacked[2], ('wide', 'narrow'), scatter_dimension=1, til...  209 us
    unnamed x3, blocking collectives  82.3 us
    all_gather x1, waiting for transfers between devices, on_device(): lax.all_gather(expand_weight.astype(jnp.bfloat16), ('wide', 'narrow'), ax...  81.8 us
    all_gather x1, waiting for transfers between devices, on_device(): lax.all_gather(shrink_weight.astype(jnp.bfloat16), ('wide', 'narrow'), ax...  80.1 us
    reduce_scatter x1, waiting for transfers between devices, on_device(): lax.psum_scatter(stacked[0], ('wide', 'narrow'), scatter_dimension=1, til...  78.6 us
    all_gather x1, waiting for transfers between devices, on_device(): lax.all_gather(embed_table.astype(jnp.bfloat16), ('wide', 'narrow'), axis...  68.1 us
  transfers between devices with their start and end apart: 10, of which 9 were waited for; matrix products, arithmetic and copies ran while one was open for 10% of the time, Pallas kernels for 0%

commit v1 on v0

v1 whole, which is shorter than its diff:
```python
import jax
import jax.numpy as jnp
from jax import lax
from jax.sharding import PartitionSpec as P

D = 768
H = 12
HD = 64
FF = 3072
V = 18000
LP = 384
LQ = 32
LANE = 128
VALID_PER_QUERY = 5

MARGIN = 1.0
CLIP = 1.0
BETA_ONE = 0.9
BETA_TWO = 0.999
LEARN_RATES = (1.0, 0.02, 0.08, 0.02, 0.02, 1.0, 0.1)
WEIGHT_DECAY = 0.01
ADAM_EPS = 1e-08
NORM_EPS = 1e-05
AXES = ("wide", "narrow")
F32 = jnp.float32
BF16 = jnp.bfloat16
O_Q, O_V, O_O, O_1, O_IN, O_OUT, O_2, O_EMB = (
    0, D, 2 * D, 3 * D, 4 * D, 4 * D + FF, 5 * D + FF, 6 * D + FF
)


def dot(left, right, dims):
    return lax.dot_general(left, right, (dims, ((), ())), preferred_element_type=F32)


def norm_rows(values, gain, shift):
    center = values - jnp.mean(values, axis=-1, keepdims=True)
    spread = jnp.mean(center * center, axis=-1, keepdims=True)
    scale = lax.rsqrt(spread + NORM_EPS)
    hat = center * scale
    return hat * gain + shift, hat, scale


def norm_rows_back(grad, gain, hat, scale):
    scaled = grad * gain
    mean_one = jnp.mean(scaled, axis=-1, keepdims=True)
    mean_two = jnp.mean(scaled * hat, axis=-1, keepdims=True)
    return scale * (scaled - mean_one - hat * mean_two)


def gelu_both(upper):
    cdf = 0.5 * (1.0 + lax.erf(upper * 0.7071067811865476))
    pdf = jnp.exp(-0.5 * upper * upper) * 0.3989422804014327
    return upper * cdf, cdf + upper * pdf


def adam_update(weight, grad, first, second, step, rate):
    first_new = BETA_ONE * first + (1.0 - BETA_ONE) * grad
    second_new = BETA_TWO * second + (1.0 - BETA_TWO) * grad * grad
    first_hat = first_new / (1.0 - BETA_ONE**step)
    second_hat = second_new / (1.0 - BETA_TWO**step)
    weight_new = weight - rate * (
        first_hat / (jnp.sqrt(second_hat) + ADAM_EPS) + WEIGHT_DECAY * weight
    )
    return (weight_new, first_new, second_new)


def gather_axes(value, axis=0):
    return lax.all_gather(value, AXES, axis=axis, tiled=False)


def exchange(blocks):
    return lax.all_to_all(blocks, AXES, 0, 0, tiled=False)


def head_mask(dtype):
    rows = lax.broadcasted_iota(jnp.int32, (H, D), 0)
    cols = lax.broadcasted_iota(jnp.int32, (H, D), 1)
    return (cols // HD == rows).astype(dtype)


def spread_heads(row):
    return row[None, :] * head_mask(row.dtype)


def table_rows(table_t, ids):
    return jnp.take(table_t, ids, axis=1)


def table_sums(values_t, ids, size):
    return jax.ops.segment_sum(values_t.T.astype(F32), ids, num_segments=size).T


def encode_front(emb_t, w_in, w_out, gain, bias, length):
    width = emb_t.shape[1]
    center = emb_t - jnp.mean(emb_t, axis=0, keepdims=True)
    spread = jnp.mean(center * center, axis=0, keepdims=True)
    scale = lax.rsqrt(spread + NORM_EPS)
    hat = center * scale
    x0 = hat * gain[0][:, None] + bias[O_EMB : O_EMB + D][:, None]
    x_low = x0.astype(BF16)
    first_low = x_low[:, 0]
    q = (dot(first_low[None], w_in[:, :D], ((1,), (0,)))[0] + bias[O_Q : O_Q + D]).astype(BF16)
    k = dot(w_in[:, D : 2 * D], x_low, ((0,), (0,))).astype(BF16)
    v = (
        dot(w_in[:, 2 * D :], x_low, ((0,), (0,))) + bias[O_V : O_V + D][:, None]
    ).astype(BF16)
    q_heads = spread_heads(q)
    s = dot(q_heads, k, ((1,), (0,))) * 0.125
    if length < width:
        live = lax.broadcasted_iota(jnp.int32, (1, width), 1) < length
        s = jnp.where(live, s, -1e30)
    peak = jnp.max(s, axis=1, keepdims=True)
    e = jnp.exp(s - peak)
    p = e / jnp.sum(e, axis=1, keepdims=True)
    p_low = p.astype(BF16)
    mixed = dot(p_low, v, ((1,), (1,)))
    a = jnp.sum(mixed * head_mask(F32), axis=0).astype(BF16)
    o = dot(a[None], w_out, ((1,), (0,)))[0] + bias[O_O : O_O + D]
    return x0[:, 0] + o, (hat, scale, x_low, q, k, v, p, p_low, a)


def encode_back(kept, row_grad, w_in, w_out, gain):
    hat, scale, x_low, q, k, v, p, p_low, a = kept
    do = row_grad.astype(BF16)
    da = dot(do[None], w_out, ((1,), (1,)))[0].astype(BF16)
    da_heads = spread_heads(da)
    q_heads = spread_heads(q)
    dp = dot(da_heads, v, ((1,), (0,)))
    ds = (p * (dp - jnp.sum(dp * p, axis=1, keepdims=True))).astype(BF16)
    dq_heads = dot(ds, k, ((1,), (1,)))
    dq = (jnp.sum(dq_heads * head_mask(F32), axis=0) * 0.125).astype(BF16)
    t = dot(ds, x_low, ((1,), (1,))) * 0.125
    w = dot(p_low, x_low, ((1,), (1,)))
    gk = (dot(q_heads, w_in[:, D : 2 * D], ((1,), (1,))) * 0.125).astype(BF16)
    ev = dot(da_heads, w_in[:, 2 * D :], ((1,), (1,))).astype(BF16)
    gx = dot(gk, ds, ((0,), (0,))) + dot(ev, p_low, ((0,), (0,)))
    first = row_grad + dot(dq[None], w_in[:, :D], ((1,), (1,)))[0]
    is_first = lax.broadcasted_iota(jnp.int32, (1, gx.shape[1]), 1) == 0
    gx = gx + jnp.where(is_first, first[:, None], 0.0)
    p_sum = jnp.sum(p_low.astype(F32), axis=1)
    dbv = jnp.repeat(p_sum, HD) * da.astype(F32)
    g_gain = jnp.sum(gx * hat, axis=1)
    g_shift = jnp.sum(gx, axis=1)
    scaled = gx * gain[0][:, None]
    mean_one = jnp.mean(scaled, axis=0, keepdims=True)
    mean_two = jnp.mean(scaled * hat, axis=0, keepdims=True)
    g_emb = scale * (scaled - mean_one - hat * mean_two)
    return g_emb, (t.astype(BF16), w.astype(BF16), q, da, dq, dbv, g_gain, g_shift)


def on_device(
    passage_ids, query_ids, passage_query, kept_mask, neg_count, step_count,
    embed_table, attend_in, attend_out, expand_weight, shrink_weight, norm_gains, bias_terms,
    embed_first, embed_second, attend_in_first, attend_in_second,
    attend_out_first, attend_out_second, expand_first, expand_second,
    shrink_first, shrink_second, gains_first, gains_second, bias_first, bias_second,
):
    narrow = lax.axis_size("narrow")
    nd = lax.axis_size("wide") * narrow
    me = lax.axis_index("wide") * narrow + lax.axis_index("narrow")
    cols = embed_table.shape[1]
    n_slots = passage_query.shape[0]
    nq = query_ids.shape[0] * lax.axis_size("wide")
    n_valid = VALID_PER_QUERY * nq
    cap = -(-n_valid // nd)
    rows_p = cap * nd
    ff_cols = FF // nd

    pid = lax.all_gather(passage_ids, AXES, axis=0, tiled=True)[:n_valid]
    qid = lax.all_gather(query_ids, "wide", axis=0, tiled=True)
    qid_pad = jnp.pad(qid, ((0, 0), (0, LANE - LQ)))
    all_ids = jnp.concatenate([pid.reshape(-1), qid_pad.reshape(-1)])

    table_t = embed_table.T
    table_low = table_t.astype(BF16)
    got = table_rows(table_low, all_ids)
    got_p = got[:, : n_valid * LP].reshape(cols, n_valid, LP)
    got_p = jnp.pad(got_p, ((0, 0), (0, rows_p - n_valid), (0, 0)))
    got_p = got_p.reshape(cols, cap, nd, LP).transpose(2, 0, 1, 3).reshape(nd, cols, cap * LP)
    got_q = got[:, n_valid * LP :].reshape(cols, nq, LANE).transpose(1, 0, 2)
    got_q = jnp.pad(got_q, ((nd - nq, 0), (0, 0), (0, 0)))
    mine = exchange(jnp.concatenate([got_p, got_q], axis=2)).reshape(D, cap * LP + LANE)
    pos = lax.all_gather(table_low[:, V : V + LP], AXES, axis=0, tiled=True).astype(F32)

    w_in = lax.all_gather(attend_in.astype(BF16), AXES, axis=1, tiled=True)
    w_out = lax.all_gather(attend_out.astype(BF16), AXES, axis=1, tiled=True)
    gains = lax.all_gather(norm_gains.astype(BF16), AXES, axis=2, tiled=True).astype(F32)
    bias = lax.all_gather(bias_terms.astype(BF16), AXES, axis=1, tiled=True).astype(F32)
    w_up = exchange(
        expand_weight.astype(BF16).reshape(2, cols, nd, ff_cols).transpose(2, 0, 1, 3)
    )
    w_up = w_up.transpose(1, 0, 2, 3).reshape(2, D, ff_cols)
    w_down = shrink_weight.astype(BF16)

    fronts = []
    for c in range(cap):
        emb = mine[:, c * LP : (c + 1) * LP].astype(F32) + pos
        fronts.append(encode_front(emb, w_in[1], w_out[1], gains[1], bias[1], LP))
    emb = mine[:, cap * LP :].astype(F32) + pos[:, :LANE]
    fronts.append(encode_front(emb, w_in[0], w_out[0], gains[0], bias[0], LQ))
    rows = gather_axes(jnp.stack([f[0] for f in fronts]))
    row_in = (rows[nd - nq :, cap], rows[:, :cap].transpose(1, 0, 2).reshape(rows_p, D))

    mids, ups = [], []
    partial_y = []
    b_in_all = bias[:, O_IN : O_IN + FF].reshape(2, nd, ff_cols)
    b_in = lax.dynamic_index_in_dim(b_in_all, me, 1, False)
    for e in range(2):
        h, hat1, scale1 = norm_rows(row_in[e], gains[e, 1], bias[e, O_1 : O_1 + D])
        h_low = h.astype(BF16)
        upper = dot(h_low, w_up[e], ((1,), (0,))) + b_in[e]
        active, slope = gelu_both(upper)
        f_low = active.astype(BF16)
        partial_y.append(dot(f_low, w_down[e], ((1,), (0,))))
        mids.append((h, hat1, scale1, h_low))
        ups.append((f_low, slope))
    y_all = lax.psum(jnp.concatenate(partial_y), AXES)
    y = (y_all[:nq], y_all[nq:])
    tops = []
    vecs = []
    for e in range(2):
        z, hat2, scale2 = norm_rows(
            mids[e][0] + y[e] + bias[e, O_OUT : O_OUT + D], gains[e, 2], bias[e, O_2 : O_2 + D]
        )
        tops.append((hat2, scale2))
        vecs.append(z.astype(BF16))
    qvec, pvec = vecs

    owner = passage_query[:rows_p]
    kept = kept_mask[:rows_p] == 1
    earlier = jnp.concatenate([jnp.full((1,), -1, jnp.int32), owner[:-1]])
    valid = owner >= 0
    first = valid & (owner != earlier)
    member = owner[None, :] == jnp.arange(nq, dtype=jnp.int32)[:, None]
    positive = member & first[None, :]
    negative = member & jnp.logical_not(first)[None, :] & kept[None, :]
    counts = jnp.sum(member.astype(F32), axis=1) - 1.0
    score_scale = 2.0 * D ** (-0.5)
    scores = dot(qvec, pvec, ((1,), (1,))) * score_scale
    masked = jnp.where(valid[None, :], scores, -1e30)
    peak = jnp.max(masked, axis=1)
    summed = jnp.sum(jnp.where(valid[None, :], jnp.exp(masked - peak[:, None]), 0.0), axis=1)
    logsum = peak + jnp.log(summed)
    pos_score = jnp.sum(jnp.where(positive, scores, 0.0), axis=1)
    margins = MARGIN - pos_score[:, None] + scores
    active_neg = negative & (margins > 0)
    hinge = jnp.sum(jnp.where(active_neg, margins, 0.0), axis=1) / counts
    active_total = jnp.sum(active_neg.astype(F32), axis=1)
    loss = jnp.sum(logsum - pos_score + hinge)
    score_grad = (
        jnp.where(valid[None, :], jnp.exp(scores - logsum[:, None]), 0.0)
        - positive.astype(F32) * (1.0 + active_total / counts)[:, None]
        + active_neg.astype(F32) / counts[:, None]
    )
    score_low = score_grad.astype(BF16)
    vec_grads = (
        (dot(score_low, pvec, ((1,), (0,))) * score_scale).astype(BF16).astype(F32),
        (dot(score_low, qvec, ((0,), (0,))) * score_scale).astype(BF16).astype(F32),
    )

    partial_h = []
    gain_grads = [[None] * 3 for _ in range(2)]
    shifts = [dict() for _ in range(2)]
    top_grads, shrink_grads, du_parts = [], [], []
    for e in range(2):
        hat2, scale2 = tops[e]
        gain_grads[e][2] = jnp.sum(vec_grads[e] * hat2, axis=0)
        shifts[e]["2"] = jnp.sum(vec_grads[e], axis=0)
        g_top = norm_rows_back(vec_grads[e], gains[e, 2], hat2, scale2)
        dy = g_top.astype(BF16)
        shifts[e]["out"] = jnp.sum(dy.astype(F32), axis=0)
        f_low, slope = ups[e]
        shrink_grads.append(dot(f_low, dy, ((0,), (0,))))
        df = dot(dy, w_down[e], ((1,), (1,)))
        du = (slope * df).astype(BF16)
        du_parts.append(du)
        partial_h.append(dot(du, w_up[e], ((1,), (1,))))
        top_grads.append(g_top)
    h_all = lax.psum(jnp.concatenate(partial_h), AXES)
    h_back = (h_all[:nq], h_all[nq:])
    du_all = gather_axes(jnp.concatenate(du_parts))
    du_all = du_all.transpose(1, 0, 2).reshape(nq + rows_p, FF)
    do_rows, expand_grads, mid_grads = [], [], []
    for e in range(2):
        h, hat1, scale1, h_low = mids[e]
        du_full = du_all[:nq] if e == 0 else du_all[nq:]
        shifts[e]["in"] = jnp.sum(du_full.astype(F32), axis=0)
        h_cols = lax.dynamic_slice_in_dim(h_low, me * cols, cols, 1)
        expand_grads.append(dot(h_cols, du_full, ((0,), (0,))))
        g_h = top_grads[e] + h_back[e]
        gain_grads[e][1] = jnp.sum(g_h * hat1, axis=0)
        shifts[e]["1"] = jnp.sum(g_h, axis=0)
        g_mid = norm_rows_back(g_h, gains[e, 1], hat1, scale1)
        mid_grads.append(g_mid)
        do_low = g_mid.astype(BF16)
        do_rows.append(do_low)
        shifts[e]["o"] = jnp.sum(do_low.astype(F32), axis=0)

    mine_p = lax.dynamic_index_in_dim(mid_grads[1].reshape(cap, nd, D), me, 1, False)
    q_at = jnp.clip(me - (nd - nq), 0, nq - 1)
    q_live = (me >= nd - nq).astype(F32)
    mine_q = lax.dynamic_index_in_dim(mid_grads[0], q_at, 0, False) * q_live
    backs = [
        encode_back(fronts[c][1], mine_p[c], w_in[1], w_out[1], gains[1]) for c in range(cap)
    ]
    backs.append(encode_back(fronts[cap][1], mine_q, w_in[0], w_out[0], gains[0]))

    send = jnp.concatenate([b[0] for b in backs], axis=1).astype(BF16).reshape(nd, cols, -1)
    came = exchange(send)
    came_p = came[:, :, : cap * LP].reshape(nd, cols, cap, LP).transpose(1, 2, 0, 3)
    came_p = came_p.reshape(cols, rows_p, LP)[:, :n_valid]
    came_q = came[nd - nq :, :, cap * LP :].transpose(1, 0, 2)
    token_grads = jnp.concatenate(
        [came_p.reshape(cols, n_valid * LP), came_q.reshape(cols, nq * LANE)], axis=1
    )
    table_grad = table_sums(token_grads, all_ids, V + LP)
    pos_grad = jnp.sum(came_p.astype(F32), axis=1)
    pos_grad = pos_grad.at[:, :LANE].add(jnp.sum(came_q.astype(F32), axis=1))
    table_grad = table_grad.at[:, V:].add(pos_grad)

    def by_columns(pick):
        stacked = jnp.stack([pick(i) for i in range(cap + 1)])
        r = stacked.shape[1]
        return exchange(stacked.reshape(cap + 1, r, nd, cols).transpose(2, 0, 1, 3))

    t_all = by_columns(lambda i: backs[i][1][0])
    w_all = by_columns(lambda i: backs[i][1][1])
    x_all = by_columns(lambda i: fronts[i][1][2][:, 0][None])[:, :, 0]
    a_all = by_columns(lambda i: fronts[i][1][8][None])[:, :, 0]
    q_all = gather_axes(jnp.stack([b[1][2] for b in backs]))
    da_all = gather_axes(jnp.stack([b[1][3] for b in backs]))
    dq_all = gather_axes(jnp.stack([b[1][4] for b in backs]))

    def of_encoder(value, e):
        if e == 0:
            return value[nd - nq :, cap]
        return value[:, :cap].reshape((nd * cap,) + value.shape[2:])

    in_grads, out_grads = [], []
    for e in range(2):
        t, w, x, a = (of_encoder(u, e) for u in (t_all, w_all, x_all, a_all))
        q, da, dq = (of_encoder(u, e) for u in (q_all, da_all, dq_all))
        rows_e = q.shape[0]
        qh = q.reshape(rows_e, H, HD)
        dah = da.reshape(rows_e, H, HD)
        g_q = dot(x, dq, ((0,), (0,)))
        g_k = jnp.einsum("phi,phd->ihd", t, qh, preferred_element_type=F32).reshape(cols, D)
        g_v = jnp.einsum("phi,phd->ihd", w, dah, preferred_element_type=F32).reshape(cols, D)
        in_grads.append(jnp.concatenate([g_q, g_k, g_v], axis=1))
        do_e = do_rows[e] if e == 0 else do_rows[e].reshape(cap, nd, D).transpose(1, 0, 2).reshape(nd * cap, D)
        out_grads.append(dot(a, do_e, ((0,), (0,))))
        shifts[e]["q"] = jnp.sum(dq.astype(F32), axis=0)
    small = jnp.stack(
        [
            jnp.stack([backs[cap][1][j] for j in (5, 6, 7)]),
            jnp.stack([sum(backs[c][1][j] for c in range(cap)) for j in (5, 6, 7)]),
        ]
    )
    small = lax.psum(small, AXES)
    gain_grad = jnp.stack([jnp.stack([small[e, 1], gain_grads[e][1], gain_grads[e][2]]) for e in range(2)])
    bias_grad = jnp.stack(
        [
            jnp.concatenate(
                [shifts[e]["q"], small[e, 0], shifts[e]["o"], shifts[e]["1"], shifts[e]["in"],
                 shifts[e]["out"], shifts[e]["2"], small[e, 2]]
            )
            for e in range(2)
        ]
    )
    grads = (
        table_grad.T,
        jnp.stack(in_grads),
        jnp.stack(out_grads),
        jnp.stack(expand_grads),
        jnp.stack(shrink_grads),
        lax.dynamic_slice_in_dim(gain_grad, me * cols, cols, 2),
        lax.dynamic_slice_in_dim(bias_grad, me * bias_terms.shape[1], bias_terms.shape[1], 1),
    )
    local_squares = sum(jnp.sum(g * g) for g in grads)
    grad_norm = jnp.sqrt(lax.psum(local_squares, AXES))
    factor = CLIP / jnp.maximum(grad_norm, CLIP)
    step = step_count[0].astype(F32)
    masters = (embed_table, attend_in, attend_out, expand_weight, shrink_weight, norm_gains, bias_terms)
    firsts = (embed_first, attend_in_first, attend_out_first, expand_first, shrink_first, gains_first, bias_first)
    seconds = (embed_second, attend_in_second, attend_out_second, expand_second, shrink_second, gains_second, bias_second)
    results = [loss, grad_norm]
    for index in range(7):
        results.extend(
            adam_update(masters[index], grads[index] * factor, firsts[index], seconds[index], step, LEARN_RATES[index])
        )
    return tuple(results)


def solution(mesh):
    both = ("wide", "narrow")
    weight_specs = (P(None, both),) + (P(None, both, None),) * 4 + (P(None, None, both), P(None, both))
    pairs = tuple(s for spec in weight_specs for s in (spec, spec))
    in_specs = (P(both, None), P("wide", None), P(), P(), P("wide"), P()) + weight_specs + pairs
    out_specs = (P(), P()) + tuple(s for spec in weight_specs for s in (spec, spec, spec))
    return jax.shard_map(on_device, mesh=mesh, in_specs=in_specs, out_specs=out_specs, check_vma=False)
```

time: 2350 us -> 1250 us (0.53)
  waiting for transfers between devices: 1600 us -> 231 us
  blocking collectives: 256 us -> 479 us
  local copies, waits for them, and re-layouts: 123 us -> 218 us
  matrix products: 150 us -> 70.8 us
  starting transfers between devices: 0.42 us -> 32.3 us
    unnamed x11 -> x4, waiting for transfers between devices: 803 us -> 0.09 us
    reduce_scatter x4 -> x0, waiting for transfers between devices: 497 us -> none  [the longest x1 209 us: on_device(): lax.psum_scatter(stacked[3], ('wide', 'narrow'), scatter_dimension=1, til...]
    all_gather x5 -> x2, waiting for transfers between devices: 303 us -> 0.02 us  [the longest x1 0.02 us: on_device(): w_in = lax.all_gather(attend_in.astype(BF16), AXES, axis=1, tiled=True)]
    all_gather x3 -> x10, blocking collectives: 115 us -> 404 us  [the longest x5 207 us: gather_axes(): return lax.all_gather(value, AXES, axis=axis, tiled=False)]
    psum x0 -> x2, waiting for transfers between devices: none -> 199 us  [the longest x1 106 us: on_device(): h_all = lax.psum(jnp.concatenate(partial_h), AXES)]
    unnamed x3 -> x0, blocking collectives: 82.3 us -> none
    dot_general x38 -> x65, matrix products: 150 us -> 70.8 us  [the longest x61 69.9 us: dot(): lax.dot_general(left, right, (dims, ((), ())), preferred_element_type=F32)]
    scatter-add x3 -> x2, other arithmetic: 38.9 us -> 93.5 us  [the longest x1 92.8 us: table_sums(): return jax.ops.segment_sum(values_t.T.astype(F32), ids, num_segments=size).T]
  transfers between devices with their start and end apart: 10 -> 11, of which waited for: 9 -> 5; matrix products, arithmetic and copies ran while one was open for 10% -> 16% of each run, Pallas kernels for 0% -> 0%
where the time goes in v1:
time: 1250 us; the launch traced here: 1240 us
  blocking collectives  479 us (38%)
  waiting for transfers between devices  231 us (18%)
  local copies, waits for them, and re-layouts  218 us (17%)
  other arithmetic  181 us (14%)
  matrix products  70.8 us (6%)
  starting transfers between devices  32.3 us (3%)
  between operations  23.7 us (2%)
    all_gather x5, blocking collectives, gather_axes(): return lax.all_gather(value, AXES, axis=axis, tiled=False)  207 us
    psum x1, waiting for transfers between devices, on_device(): h_all = lax.psum(jnp.concatenate(partial_h), AXES)  106 us
    psum x1, waiting for transfers between devices, on_device(): y_all = lax.psum(jnp.concatenate(partial_y), AXES)  93.7 us
    scatter-add x1, other arithmetic, table_sums(): return jax.ops.segment_sum(values_t.T.astype(F32), ids, num_segments=size).T  92.8 us
    dot_general x61, matrix products, dot(): lax.dot_general(left, right, (dims, ((), ())), preferred_element_type=F32)  69.9 us
    all_gather x1, blocking collectives, on_device(): lax.all_gather(bias_terms.astype(BF16), AXES, axis=1, tiled=True)  58.6 us
    gather x1, local copies, waits for them, and re-layouts, table_rows(): return jnp.take(table_t, ids, axis=1)  57.9 us
    all_gather x1, blocking collectives, on_device(): pid = lax.all_gather(passage_ids, AXES, axis=0, tiled=True)[:n_valid]  43.7 us
  transfers between devices with their start and end apart: 11, of which 5 were waited for; matrix products, arithmetic and copies ran while one was open for 16% of the time, Pallas kernels for 0%

profile of v1, /device:TPU:0, one launch (start us, length us, event | category | flops | bytes accessed | tf_op | source)
XLA Modules:
  0.0 1235.5 jit_solution(8759387920847731818)
XLA Ops:
  10.4 7.4 all-to-all-start.1
  17.9 43.7 %all-gather.5 = s32[32,2,384]{2,1,0:T(2,128)S(1)} all-gather(s32[1,2,384]{2,1,0:T(2,128)S(1)} %bitcast.338), channel_id=1, replica_groups=mesh['wide'=8,'narrow'=4] {'wide','narrow'}, dimensions={0}, use_global_device_ids=true | all-gather | bytes 101376 | tf_op jit(solution)/shard_map/all_gather | solution.py:170
  61.9 3.4 copy.261
  65.3 16.7 %all-gather.6 = s32[8,1,32]{2,1,0:T(1,128)S(1)} all-gather(s32[1,1,32]{2,1,0:T(1,128)S(1)} %bitcast.339), channel_id=1, replica_groups=mesh['wide'=8,'narrow'=4] {'wide'}, dimensions={0}, use_global_device_ids=true | all-gather | bytes 1152 | tf_op jit(solution)/shard_map/all_gather | solution.py:171
  82.1 57.9 %gather_fusion = bf16[16384,24]{1,0:T(8,128)(2,1)} fusion(bf16[24,18384]{0,1:T(8,128)(2,1)} %copy.261, s32[16384]{0:T(1024)S(1)} %broadcast_clamp_fusion), kind=kCustom, calls=%fused_computation | custom fusion | bytes 1638400 | tf_op jit(solution)/shard_map/jit(_take)/gather | solution.py:87
  140.0 10.9 select_bitcast_fusion
  152.9 4.4 pad.17
  157.3 6.1 copy.262
  165.7 3.5 all-to-all-start
  170.0 58.6 %all-gather.7 = bf16[32,264,2]{1,2,0:T(2,128)(2,1)S(1)} all-gather(bf16[1,264,2]{1,2,0:T(2,128)(2,1)S(1)} %convert_bitcast_fusion.2), channel_id=1, replica_groups=mesh['wide'=8,'narrow'=4] {'wide','narrow'}, dimensions={0}, use_global_device_ids=true | all-gather | bytes 34848 | tf_op jit(solution)/shard_map/all_gather | solution.py:189
  228.9 39.2 %all_gather.54 = bf16[2,3,768]{1,0,2:T(2,128)(2,1)S(1)} all-gather(bf16[2,3,24]{1,0,2:T(2,128)(2,1)S(1)} %copy.264), channel_id=1, replica_groups=mesh['wide'=8,'narrow'=4] {'wide','narrow'}, dimensions={2}, use_global_device_ids=true | all-gather | bytes 9504 | tf_op jit(solution)/shard_map/all_gather | solution.py:188
  268.5 38.9 %all_gather.53 = bf16[768,384]{1,0:T(8,128)(2,1)S(1)} all-gather(bf16[24,384]{1,0:T(8,128)(2,1)S(1)} %slice.469), channel_id=1, replica_groups=mesh['wide'=8,'narrow'=4] {'wide','narrow'}, dimensions={0}, use_global_device_ids=true | all-gather | bytes 608256 | tf_op jit(solution)/shard_map/all_gather | solution.py:184
  314.7 13.1 %slice_reduce_fusion.1 = (f32[768]{0:T(1024)}, f32[768]{0:T(1024)}, f32[768]{0:T(1024)S(1)}, f32[768]{0:T(1024)}, f32[768]{0:T(1024)}, /*index=5*/f32[768]{0:T(1024)S(1)}) fusion(f32[2,3,768]{1,0,2:T(2,128)S(1)} %convert_element_type.440), kind=kLoop, calls=%fused_computation.173 | loop fusion | bytes 36864 | tf_op jit(solution)/shard_map/slice | solution.py:224
  334.5 2.7 all-to-all-start.3
  340.9 3.6 all-to-all-done.3
  345.3 3.5 slice_bitcast_fusion.1
  370.2 39.4 %all-gather.8 = f32[32,3,768]{2,1,0:T(4,128)S(1)} all-gather(f32[1,3,768]{2,1,0:T(4,128)S(1)} %maximum_bitcast_fusion.6), channel_id=2, replica_groups=mesh['wide'=8,'narrow'=4] {'wide','narrow'}, dimensions={0}, use_global_device_ids=true | all-gather | bytes 304128 | tf_op jit(solution)/shard_map/all_gather | solution.py:69
  415.6 2.1 convolution_convert_fusion.8
  417.7 2.0 convolution_convert_fusion.7
  424.5 3.2 all-to-all-start.6
  436.5 44.9 %all-gather.10 = bf16[32,3,768]{2,1,0:T(4,128)(2,1)} all-gather(bf16[1,3,768]{2,1,0:T(4,128)(2,1)S(1)} %maximum_bitcast_fusion.12), channel_id=4, replica_groups=mesh['wide'=8,'narrow'=4] {'wide','narrow'}, dimensions={0}, use_global_device_ids=true | all-gather | bytes 152064 | tf_op jit(solution)/shard_map/all_gather | solution.py:69
  495.4 2.0 reshape.973
  499.0 3.3 all-to-all-start.5
  513.0 93.7 %all-reduce.6.cloned.1.call-done = f32[72,768]{1,0:T(8,128)} async-done(((f32[72,768]{1,0:T(8,128)}), f32[72,768]{1,0:T(8,128)}) %all-reduce.6.cloned.1.call-update) | async-done | bytes 221200 | tf_op jit(solution)/shard_map/psum | solution.py:218
  619.5 43.3 %all-gather.4 = bf16[2304,96]{1,0:T(8,128)(2,1)S(1)} all-gather(bf16[72,96]{1,0:T(8,128)(2,1)S(1)} %pad_maximum_fusion.8), channel_id=6, replica_groups=mesh['wide'=8,'narrow'=4] {'wide','narrow'}, dimensions={0}, use_global_device_ids=true | all-gather | bytes 456192 | tf_op jit(solution)/shard_map/all_gather | solution.py:69
  675.3 2.5 slice.455
  683.6 105.8 %all-reduce.8.cloned.1.call-done = f32[72,768]{1,0:T(8,128)} async-done(((f32[72,768]{1,0:T(8,128)}), f32[72,768]{1,0:T(8,128)}) %all-reduce.8.cloned.1.call-update) | async-done | bytes 221200 | tf_op jit(solution)/shard_map/psum | solution.py:280
  796.3 2.7 fusion.27
  804.0 2.3 convert_reduce_fusion.3
  809.4 2.5 fusion.29
  819.0 2.5 fusion.28
  825.0 42.0 %all-gather.9 = bf16[32,3,768]{2,1,0:T(4,128)(2,1)S(1)} all-gather(bf16[1,3,768]{2,1,0:T(4,128)(2,1)S(1)} %maximum_bitcast_fusion.11), channel_id=3, replica_groups=mesh['wide'=8,'narrow'=4] {'wide','narrow'}, dimensions={0}, use_global_device_ids=true | all-gather | bytes 152064 | tf_op jit(solution)/shard_map/all_gather | solution.py:69
  872.7 37.2 %all-gather.11 = bf16[32,3,768]{2,1,0:T(4,128)(2,1)S(1)} all-gather(bf16[1,3,768]{2,1,0:T(4,128)(2,1)S(1)} %maximum_bitcast_fusion.13), channel_id=5, replica_groups=mesh['wide'=8,'narrow'=4] {'wide','narrow'}, dimensions={0}, use_global_device_ids=true | all-gather | bytes 152064 | tf_op jit(solution)/shard_map/all_gather | solution.py:69
  914.2 3.6 multiply_reduce_fusion.12
  924.4 3.1 fusion.6
  927.5 5.0 multiply_reduce_fusion.2
  935.4 37.5 %psum.30 = f32[2,3,768]{2,1,0:T(4,128)S(1)} all-reduce(f32[2,3,768]{2,1,0:T(4,128)S(1)} %pad_maximum_fusion.7), channel_id=1, replica_groups=mesh['wide'=8,'narrow'=4] {'wide','narrow'}, use_global_device_ids=true, to_apply=%region_70.71 | all-reduce | flops 4608 | bytes 36864 | tf_op jit(solution)/shard_map/psum | solution.py:360
  1005.1 2.0 reshape.975
  1007.1 6.2 all-to-all-start.4
  1019.3 2.1 multiply_convert_fusion.1
  1022.6 5.8 all-to-all-start.2
  1035.3 26.4 %all-to-all-done.2 = bf16[32,24,896]{2,1,0:T(8,128)(2,1)S(1)} async-done(((bf16[32,24,896]{2,1,0:T(8,128)(2,1)}), bf16[32,24,896]{2,1,0:T(8,128)(2,1)S(1)}, u32[]{:S(2)}, u32[]{:S(2)}) %all-to-all-start.2) | async-done | bytes 1376288 | tf_op jit(solution)/shard_map/all_to_all | solution.py:73
  1065.1 4.7 copy.271
  1069.7 92.8 %scatter_custom_fusion = f32[18384,24]{1,0:T(8,128)} fusion(s32[16384]{0:T(1024)} %pad_add_fusion, f32[16384,24]{1,0:T(8,128)} %copy.271, f32[]{:T(128)} %constant.277.clone.1), kind=kCustom, calls=%fused_computation.2 | custom fusion | flops 393216 | bytes 1765376 | tf_op jit(solution)/shard_map/scatter-add | solution.py:91
  1162.6 5.5 copy.272
  1175.0 37.9 %psum.31 = f32[]{:T(128)} all-reduce(f32[]{:T(128)S(6)} %add.687), channel_id=1, replica_groups=mesh['wide'=8,'narrow'=4] {'wide','narrow'}, use_global_device_ids=true, to_apply=%region_89.90 | all-reduce | flops 1 | bytes 8 | tf_op jit(solution)/shard_map/psum | solution.py:381
  1215.5 3.1 multiply_subtract_fusion
  1223.8 3.3 add_subtract_fusion
  (716 shorter events, 227.7 us)
Async XLA Ops:
  7.2 338.0 %all-gather.15.cloned.1.call-start = ((), (), s32[]{:S(2)}) async-start(), calls=%async_computation.7 | async-start | bytes 7299072 | tf_op jit(solution)/shard_map/all_gather | solution.py:186
  9.5 52.3 %copy-start.7 = (f32[18384,24]{0,1:T(8,128)S(1)}, f32[18384,24]{0,1:T(8,128)}, u32[]{:S(2)}) copy-start(f32[18384,24]{0,1:T(8,128)} %param.36) | copy-start | bytes 5294596
  10.4 155.3 %all-to-all-start.1 = ((bf16[32,2,24,96]{3,2,1,0:T(8,128)(2,1)}), bf16[32,2,24,96]{3,2,1,0:T(8,128)(2,1)}, u32[]{:S(2)}, u32[]{:S(2)}) async-start(bf16[32,2,24,96]{3,2,1,0:T(8,128)(2,1)} %copy.267), calls=%async_computation.1 | async-start | bytes 786432 | tf_op jit(solution)/shard_map/all_to_all | solution.py:73
  61.7 78.3 %copy-start.68 = (s32[15360]{0:T(1024)}, s32[15360]{0:T(1024)S(1)}, u32[]{:S(2)}) copy-start(s32[15360]{0:T(1024)S(1)} %concatenate.83) | copy-start | bytes 184324
  165.7 63.1 %copy-start.150 = (f32[2,3,24]{2,0,1:T(2,128)S(1)}, f32[2,3,24]{2,0,1:T(2,128)}, u32[]{:S(2)}) copy-start(f32[2,3,24]{2,0,1:T(2,128)} %param.41) | copy-start | bytes 1732
  165.7 164.0 %all-to-all-start = ((bf16[32,24,896]{2,1,0:T(8,128)(2,1)}), bf16[32,24,896]{2,1,0:T(8,128)(2,1)S(1)}, u32[]{:S(2)}, u32[]{:S(2)}) async-start(bf16[32,24,896]{2,1,0:T(8,128)(2,1)} %fusion.7), calls=%async_computation | async-start | bytes 2752512 | tf_op jit(solution)/shard_map/all_to_all | solution.py:73
  169.2 196.7 %all-gather.17.cloned.1.call-start = ((), (), s32[]{:S(2)}) async-start(), calls=%async_computation.8 | async-start | bytes 2433024 | tf_op jit(solution)/shard_map/all_gather | solution.py:187
  228.8 84.0 %copy-start.77 = (f32[8448,2]{0,1:T(2,128)}, f32[8448,2]{0,1:T(2,128)S(1)}, u32[]{:S(2)}) copy-start(f32[8448,2]{0,1:T(2,128)S(1)} %reshape.889) | copy-start | bytes 202756
  268.4 40.1 %copy-start.31 = (f32[2,96,768]{2,1,0:T(8,128)S(1)}, f32[2,96,768]{2,1,0:T(8,128)}, u32[]{:S(2)}) copy-start(f32[2,96,768]{2,1,0:T(8,128)} %param.40) | copy-start | bytes 1769476
  307.4 23.1 %copy-start.2 = (bf16[768,384]{1,0:T(8,128)(2,1)}, bf16[768,384]{1,0:T(8,128)(2,1)S(1)}, u32[]{:S(2)}) copy-start(bf16[768,384]{1,0:T(8,128)(2,1)S(1)} %all_gather.53) | copy-start | bytes 1769476
  332.9 12.3 copy-start.14
  333.0 12.2 copy-start.164
  333.1 12.1 copy-start.177
  333.4 11.8 copy-start.16
  334.5 10.0 all-to-all-start.3
  348.8 14.6 %copy-start.5 = (bf16[768,2304]{1,0:T(8,128)(2,1)}, bf16[768,2304]{1,0:T(8,128)(2,1)S(1)}, u32[]{:S(2)}) copy-start(bf16[768,2304]{1,0:T(8,128)(2,1)S(1)} %get-tuple-element.309) | copy-start | bytes 10616836
  424.5 74.5 %all-to-all-start.6 = ((bf16[32,3,1,24]{3,1,2,0:T(4,128)(2,1)}), bf16[32,3,1,24]{3,1,2,0:T(4,128)(2,1)}, u32[]{:S(2)}, u32[]{:S(2)}) async-start(bf16[32,3,1,24]{3,1,2,0:T(4,128)(2,1)} %copy.294), calls=%async_computation.6 | async-start | bytes 65536 | tf_op jit(solution)/shard_map/all_to_all | solution.py:73
  427.7 179.0 %all-reduce.6.cloned.1.call-start = ((), (), s32[]{:S(2)}) async-start(), calls=%async_computation.9 | async-start | bytes 442368 | tf_op jit(solution)/shard_map/psum | solution.py:218
  499.0 10.7 all-to-all-start.5
  502.3 287.0 %all-reduce.8.cloned.1.call-start = ((), (), s32[]{:S(2)}) async-start(), calls=%async_computation.10 | async-start | bytes 442368 | tf_op jit(solution)/shard_map/psum | solution.py:280
  606.7 9.0 copy-start.104
  608.5 9.5 copy-start.30
  608.5 9.5 copy-start.109
  608.5 9.6 copy-start.54
  618.0 46.2 %copy-start.75 = (f32[8,768]{1,0:T(8,128)}, f32[8,768]{1,0:T(8,128)S(1)}, u32[]{:S(2)}) copy-start(f32[8,768]{1,0:T(8,128)S(1)} %get-tuple-element.276) | copy-start | bytes 73732
  619.1 46.1 %copy-start.22 = (f32[64,768]{1,0:T(8,128)}, f32[64,768]{1,0:T(8,128)S(1)}, u32[]{:S(2)}) copy-start(f32[64,768]{1,0:T(8,128)S(1)} %get-tuple-element.271) | copy-start | bytes 589828
  821.6 48.7 %copy-start.11 = (bf16[768,384]{1,0:T(8,128)(2,1)S(1)}, bf16[768,384]{1,0:T(8,128)(2,1)}, u32[]{:S(2)}) copy-start(bf16[768,384]{1,0:T(8,128)(2,1)} %copy-done.9) | copy-start | bytes 1769476
  821.6 50.3 %copy-start.19 = (bf16[768,128]{1,0:T(8,128)(2,1)S(1)}, bf16[768,128]{1,0:T(8,128)(2,1)}, u32[]{:S(2)}) copy-start(bf16[768,128]{1,0:T(8,128)(2,1)} %copy-done.16) | copy-start | bytes 589828
  821.6 50.3 %copy-start.100 = (bf16[12,128]{1,0:T(8,128)(2,1)S(1)}, bf16[12,128]{1,0:T(8,128)(2,1)}, u32[]{:S(2)}) copy-start(bf16[12,128]{1,0:T(8,128)(2,1)} %multiply_convert_fusion.6) | copy-start | bytes 9220
  821.6 51.1 %copy-start.114 = (bf16[768]{0:T(1024)(128)(2,1)S(1)}, bf16[768]{0:T(1024)(128)(2,1)}, u32[]{:S(2)}) copy-start(bf16[768]{0:T(1024)(128)(2,1)} %copy-done.113) | copy-start | bytes 4612
  821.6 51.1 %copy-start.125 = (bf16[768]{0:T(1024)(128)(2,1)S(1)}, bf16[768]{0:T(1024)(128)(2,1)}, u32[]{:S(2)}) copy-start(bf16[768]{0:T(1024)(128)(2,1)} %copy-done.124) | copy-start | bytes 4612
  824.9 86.4 %copy-start.133 = (f32[768]{0:T(1024)S(1)}, f32[768]{0:T(1024)}, u32[]{:S(2)}) copy-start(f32[768]{0:T(1024)} %reshape.843) | copy-start | bytes 9220
  870.3 43.4 %copy-start.134 = (f32[768]{0:T(1024)S(1)}, f32[768]{0:T(1024)}, u32[]{:S(2)}) copy-start(f32[768]{0:T(1024)} %fusion.280) | copy-start | bytes 9220
  927.5 66.0 %copy-start.130 = (f32[768]{0:T(1024)S(1)}, f32[768]{0:T(1024)}, u32[]{:S(2)}) copy-start(f32[768]{0:T(1024)} %get-tuple-element.270) | copy-start | bytes 9220
  986.0 33.2 %copy-start.21 = (f32[768,384]{1,0:T(8,128)S(1)}, f32[768,384]{1,0:T(8,128)}, u32[]{:S(2)}) copy-start(f32[768,384]{1,0:T(8,128)} %fusion.6) | copy-start | bytes 3538948
  993.5 19.8 %copy-start.101 = (bf16[8,768]{1,0:T(8,128)(2,1)S(1)}, bf16[8,768]{1,0:T(8,128)(2,1)}, u32[]{:S(2)}) copy-start(bf16[8,768]{1,0:T(8,128)(2,1)} %slice_reduce_fusion.12) | copy-start | bytes 36868
  998.8 19.2 %copy-start.15 = (f32[768,128]{1,0:T(8,128)S(1)}, f32[768,128]{1,0:T(8,128)}, u32[]{:S(2)}) copy-start(f32[768,128]{1,0:T(8,128)} %copy-done.14) | copy-start | bytes 1179652
  998.8 19.2 %copy-start.103 = (f32[768]{0:T(1024)S(1)}, f32[768]{0:T(1024)}, u32[]{:S(2)}) copy-start(f32[768]{0:T(1024)} %get-tuple-element.205) | copy-start | bytes 9220
  1004.2 15.1 %copy-start.1 = (bf16[32,24,896]{2,1,0:T(8,128)(2,1)S(1)}, bf16[32,24,896]{2,1,0:T(8,128)(2,1)}, u32[]{:S(2)}) copy-start(bf16[32,24,896]{2,1,0:T(8,128)(2,1)} %copy-done) | copy-start | bytes 4128772
  1004.2 15.1 %copy-start.3 = (bf16[768,384]{1,0:T(8,128)(2,1)S(1)}, bf16[768,384]{1,0:T(8,128)(2,1)}, u32[]{:S(2)}) copy-start(bf16[768,384]{1,0:T(8,128)(2,1)} %copy-done.2) | copy-start | bytes 1769476
  1007.1 15.5 %all-to-all-start.4 = ((bf16[32,2,432]{2,1,0:T(2,128)(2,1)}), bf16[32,2,432]{2,1,0:T(2,128)(2,1)}, u32[]{:S(2)}, u32[]{:S(2)}) async-start(bf16[32,2,432]{2,1,0:T(2,128)(2,1)} %reshape.975), calls=%async_computation.4 | async-start | bytes 131072 | tf_op jit(solution)/shard_map/all_to_all | solution.py:73
  1022.6 39.2 %all-to-all-start.2 = ((bf16[32,24,896]{2,1,0:T(8,128)(2,1)}), bf16[32,24,896]{2,1,0:T(8,128)(2,1)S(1)}, u32[]{:S(2)}, u32[]{:S(2)}) async-start(bf16[32,24,896]{2,1,0:T(8,128)(2,1)} %pad_maximum_fusion), calls=%async_computation.2 | async-start | bytes 2752512 | tf_op jit(solution)/shard_map/all_to_all | solution.py:73
  1034.6 27.3 %copy-start.41 = (f32[1,24,2304]{2,1,0:T(8,128)}, f32[1,24,2304]{2,1,0:T(8,128)S(1)}, u32[]{:S(2)}) copy-start(f32[1,24,2304]{2,1,0:T(8,128)S(1)} %maximum_bitcast_fusion.2) | copy-start | bytes 663556
  1168.0 45.6 %copy-start.151 = (f32[2,3,24]{2,0,1:T(2,128)S(1)}, f32[2,3,24]{2,0,1:T(2,128)}, u32[]{:S(2)}) copy-start(f32[2,3,24]{2,0,1:T(2,128)} %param.41) | copy-start | bytes 1732
  1168.1 45.6 %copy-start.173 = (f32[2,3,24]{2,0,1:T(2,128)S(1)}, f32[2,3,24]{2,0,1:T(2,128)}, u32[]{:S(2)}) copy-start(f32[2,3,24]{2,0,1:T(2,128)} %param.54) | copy-start | bytes 1732
  1168.1 45.6 %copy-start.174 = (f32[2,3,24]{2,0,1:T(2,128)S(1)}, f32[2,3,24]{2,0,1:T(2,128)}, u32[]{:S(2)}) copy-start(f32[2,3,24]{2,0,1:T(2,128)} %param.53) | copy-start | bytes 1732
  1168.1 47.4 %copy-start.23 = (f32[1,96,768]{2,1,0:T(8,128)S(1)}, f32[1,96,768]{2,1,0:T(8,128)}, u32[]{:S(2)}) copy-start(f32[1,96,768]{2,1,0:T(8,128)} %convolution_bitcast_fusion.2) | copy-start | bytes 884740
  1168.1 47.4 %copy-start.26 = (f32[1,96,768]{2,1,0:T(8,128)S(1)}, f32[1,96,768]{2,1,0:T(8,128)}, u32[]{:S(2)}) copy-start(f32[1,96,768]{2,1,0:T(8,128)} %convolution_bitcast_fusion.3) | copy-start | bytes 884740
  (148 other events, 429.1 us)
Sparse Core Ops, SparseCore 0:
  11.5 77.5 all-gather.14
  173.5 59.5 all-gather.16
  485.7 120.9 all-reduce.5
  668.5 120.7 all-reduce.7
